TPU v7x, 32 devices: a whole 2x2x4 slice. The times are simulated.
32 devices in a mesh: replica: 8 (over z, core), shard: 4 (over y, x).
Axes of the slice: x: 2, y: 2, z: 4, core: 2. Of those that a mesh axis runs over, the one named last changes fastest.
Arguments:
- local_weights: bfloat16 [8, 8192, 512], P('replica', 'shard'), may hold values from -1.3258252 to 1.3258252
- outer_base: bfloat16 [8192, 512], P('shard'), may hold values from -0.0625 to 0.0625
- momentum: bfloat16 [8192, 512], P('shard', 'replica'), may hold values from -0.06591797 to 0.06591797
- error_feedback: bfloat16 [8, 8192, 512], P('replica', 'shard'), may hold values from -0.032958984 to 0.032958984
- q_start: float32 [512, 32], replicated, may hold values from -6 to 6
- tokens: bfloat16 [8, 512, 8192], P('replica', None, 'shard'), may hold values from -6 to 6
Outputs:
- new_base: bfloat16 [8192, 512], P('shard')
- new_momentum: bfloat16 [8192, 512], P('shard', 'replica')
- new_error: bfloat16 [8, 8192, 512], P('replica', 'shard')
- key_rows: bfloat16 [8, 512, 512], P('replica', 'shard')
All inputs are finite; a program needn't handle non-finite values.
Results may differ from a plain program's by a relative error of at most 0.0065.
Values may be sent and summed in bfloat16 or wider, within the bound.
A program may use at most 64 MiB of HBM per device.

v0:
```python
import jax
import jax.numpy as jnp
from jax import lax
from jax.sharding import PartitionSpec as P

outer_mu = 0.9
outer_rate = 0.7


def on_device(local_weights, outer_base, momentum, error_feedback, q_start, tokens):
    highest = lax.Precision.HIGHEST
    replicas = lax.axis_size("replica")
    own_columns = momentum.shape[1]
    full_momentum = lax.all_gather(momentum, "replica", axis=1, tiled=True)
    pseudo = (
        outer_base.astype(jnp.float32)
        - local_weights[0].astype(jnp.float32)
        + error_feedback[0].astype(jnp.float32)
    )
    p_local = jnp.dot(pseudo, q_start, precision=highest)
    p_mean = lax.psum(p_local, "replica") / replicas
    own_gram = jnp.dot(p_mean.T, p_mean, precision=highest)
    gram_sum = lax.psum(own_gram, "shard")
    factor_low = jnp.linalg.cholesky(gram_sum)
    basis = jax.scipy.linalg.solve_triangular(factor_low, p_mean.T, lower=True).T
    q_raw = jnp.dot(pseudo.T, basis, precision=highest)
    q_mean = lax.psum(q_raw, ("replica", "shard")) / replicas
    update = jnp.dot(basis, q_mean.T, precision=highest)
    new_error = (pseudo - update).astype(jnp.bfloat16)[None]
    moment = outer_mu * full_momentum.astype(jnp.float32) + update
    new_base = (outer_base.astype(jnp.float32) - outer_rate * (outer_mu * moment + update)).astype(
        jnp.bfloat16
    )
    first_column = lax.axis_index("replica") * own_columns
    new_momentum = lax.dynamic_slice_in_dim(moment, first_column, own_columns, 1).astype(
        jnp.bfloat16
    )
    own_tokens = tokens[0]
    key_sum = lax.psum_scatter(
        jnp.dot(own_tokens, new_base, preferred_element_type=jnp.float32),
        "shard",
        scatter_dimension=0,
        tiled=True,
    )
    key_rows = key_sum.astype(jnp.bfloat16)[None]
    return (new_base, new_momentum, new_error, key_rows)


def solution(mesh):
    in_specs = (
        P("replica", "shard", None),
        P("shard", None),
        P("shard", "replica"),
        P("replica", "shard", None),
        P(),
        P("replica", None, "shard"),
    )
    out_specs = (
        P("shard", None),
        P("shard", "replica"),
        P("replica", "shard", None),
        P("replica", "shard", None),
    )
    return jax.shard_map(
        on_device, mesh=mesh, in_specs=in_specs, out_specs=out_specs, check_vma=False
    )
```

profile of v0, /device:TPU:0, one launch (start us, length us, event | category | flops | bytes accessed | tf_op | source)
XLA Modules:
  0.0 319.2 jit_solution(3947755793024692435)
XLA Ops:
  7.2 0.0 all-reduce.3.cloned.1.call-start
  7.2 4.1 %copy.10 = bf16[2048,512]{0,1:T(8,128)(2,1)} copy(bf16[2048,512]{1,0:T(8,128)(2,1)} %param.7) | data formatting | bytes 4194304 | tf_op args[1]
  11.3 4.0 %copy.11 = bf16[1,2048,512]{1,2,0:T(8,128)(2,1)} copy(bf16[1,2048,512]{2,1,0:T(8,128)(2,1)} %param.6) | data formatting | bytes 4194304 | tf_op args[0]
  15.3 3.9 %copy.12 = bf16[1,2048,512]{1,2,0:T(8,128)(2,1)} copy(bf16[1,2048,512]{2,1,0:T(8,128)(2,1)} %param.9) | data formatting | bytes 4194304 | tf_op args[3]
  19.2 6.8 %fusion.10 = f32[2048,32]{0,1:T(8,128)} fusion(f32[512,32]{0,1:T(8,128)S(1)} %copy-done.6, bf16[2048,512]{0,1:T(8,128)(2,1)} %copy.10, bf16[1,2048,512]{1,2,0:T(8,128)(2,1)} %copy.12, bf16[1,2048,512]{1,2,0:T(8,128)(2,1)} %copy.11), kind=kOutput, calls=%fused_computation.11 | convolution fusion | flops 407896064 | bytes 6619136 | tf_op jit(solution)/shard_map/dot_general | solution.py:20
  26.0 0.0 all-reduce.3.cloned.1.call-update
  26.0 0.0 all-reduce.5.cloned.1.call-start
  26.1 58.3 %all-reduce.3.cloned.1.call-done = f32[2048,32]{0,1:T(8,128)} async-done(((f32[2048,32]{0,1:T(8,128)}), f32[2048,32]{0,1:T(8,128)}) %all-reduce.3.cloned.1.call-update) | async-done | bytes 262160 | tf_op jit(solution)/shard_map/psum | solution.py:21
  84.3 1.4 fusion.16
  85.7 16.0 %psum.22 = f32[32,32]{0,1:T(8,128)S(1)} all-reduce(f32[32,32]{0,1:T(8,128)S(1)} %fusion.16), channel_id=1, replica_groups=mesh['replica'=8,'shard'=4] {'shard'}, use_global_device_ids=true, to_apply=%region_1.0 | all-reduce | flops 1024 | bytes 8192 | tf_op jit(solution)/shard_map/psum | solution.py:23
  101.7 0.1 copy.14
  101.8 2.9 cholesky.16
  104.7 0.6 compare_reduce_fusion
  105.4 0.7 fusion.21
  106.0 2.4 custom-call.7
  108.4 1.4 fusion.14
  109.8 6.4 %fusion.8 = f32[512,32]{1,0:T(8,128)} fusion(f32[32,2048]{1,0:T(8,128)S(1)} %fusion.14, bf16[2048,512]{0,1:T(8,128)(2,1)} %copy.10, bf16[1,2048,512]{1,2,0:T(8,128)(2,1)} %copy.12, bf16[1,2048,512]{1,2,0:T(8,128)(2,1)} %copy.11), kind=kOutput, calls=%fused_computation.10 | convolution fusion | flops 407896064 | bytes 6619136 | tf_op jit(solution)/shard_map/dot_general | solution.py:26
  116.3 0.0 all-gather.2.cloned.1.call-start
  116.3 0.7 all-gather.2.cloned.1.call-update
  117.0 0.2 reduce-scatter.2.cloned.1.call-start
  117.2 123.0 %all-reduce.5.cloned.1.call-done = f32[512,32]{1,0:T(8,128)} async-done(((f32[512,32]{1,0:T(8,128)}), f32[512,32]{1,0:T(8,128)}) %all-reduce.5.cloned.1.call-update) | async-done | bytes 65552 | tf_op jit(solution)/shard_map/psum | solution.py:27
  240.2 29.8 %all-gather.2.cloned.1.call-done = bf16[2048,512]{0,1:T(8,128)(2,1)} async-done(((bf16[2048,64]{0,1:T(8,128)(2,1)}), bf16[2048,512]{0,1:T(8,128)(2,1)}) %all-gather.2.cloned.1.call-update) | async-done | bytes 2097168 | tf_op jit(solution)/shard_map/all_gather | solution.py:14
  270.1 6.3 %multiply_add_fusion = (bf16[2048,512]{0,1:T(8,128)(2,1)}, f32[2048,512]{0,1:T(8,128)S(1)}) fusion(bf16[2048,512]{0,1:T(8,128)(2,1)} %all-gather.2.cloned.1.call-done, f32[32,2048]{1,0:T(8,128)S(1)} %fusion.14, f32[512,32]{1,0:T(8,128)} %all-reduce.5.cloned.1.call-done), kind=kOutput, calls=%fused_computation.5 | convolution fusion | flops 406863872 | bytes 8716288 | tf_op jit(solution)/shard_map/dot_general | solution.py:28
  276.4 3.5 %fusion.2 = (bf16[1,2048,512]{1,2,0:T(8,128)(2,1)}, bf16[2048,512]{0,1:T(8,128)(2,1)S(1)}) fusion(f32[2048,512]{0,1:T(8,128)S(1)} %get-tuple-element.11, bf16[1,2048,512]{1,2,0:T(8,128)(2,1)S(1)} %copy-done.3, bf16[1,2048,512]{1,2,0:T(8,128)(2,1)S(1)} %copy-done.2, bf16[2048,512]{0,1:T(8,128)(2,1)S(1)} %copy-done.1, bf16[2048,512]{0,1:T(8,128)(2,1)S(1)} %copy-done.4), kind=kLoop, calls=%fused_computation.6 | loop fusion | flops 15728640 | bytes 16777216 | tf_op jit(solution)/shard_map/broadcast_in_dim | solution.py:29
  279.9 1.3 copy-done.5
  281.2 2.3 fusion.5
  283.5 3.9 %copy.15 = bf16[2048,512]{1,0:T(8,128)(2,1)} copy(bf16[2048,512]{0,1:T(8,128)(2,1)} %copy-done.5) | data formatting | bytes 4194304
  287.4 4.0 %copy.16 = bf16[1,2048,512]{2,1,0:T(8,128)(2,1)} copy(bf16[1,2048,512]{1,2,0:T(8,128)(2,1)} %get-tuple-element.8) | data formatting | bytes 4194304
  291.3 1.7 dynamic-slice_convert_fusion
  293.0 17.9 %reduce-scatter.2.cloned.1.call-done = f32[128,512]{0,1:T(8,128)} async-done(((f32[512,512]{0,1:T(8,128)}), f32[128,512]{0,1:T(8,128)}) %reduce-scatter.2.cloned.1.call-update) | async-done | bytes 262160 | tf_op jit(solution)/shard_map/reduce_scatter | solution.py:39
  310.9 1.0 convert_bitcast_fusion
  311.9 0.8 copy.17
  (17 shorter events, 0.1 us)
Async XLA Ops:
  7.2 274.0 %copy-start = (bf16[1,512,2048]{2,1,0:T(8,128)(2,1)S(1)}, bf16[1,512,2048]{2,1,0:T(8,128)(2,1)}, u32[]{:S(2)}) copy-start(bf16[1,512,2048]{2,1,0:T(8,128)(2,1)} %param.11) | copy-start | bytes 6291460
  7.2 77.1 %all-reduce.3.cloned.1.call-start = ((), (), s32[]{:S(2)}) async-start(), calls=%async_computation.2 | async-start | bytes 524288 | tf_op jit(solution)/shard_map/psum | solution.py:21
  15.3 3.9 %copy-start.6 = (f32[512,32]{0,1:T(8,128)S(1)}, f32[512,32]{0,1:T(8,128)}, u32[]{:S(2)}) copy-start(f32[512,32]{0,1:T(8,128)} %param.10) | copy-start | bytes 196612
  26.0 214.2 %all-reduce.5.cloned.1.call-start = ((), (), s32[]{:S(2)}) async-start(), calls=%async_computation.3 | async-start | bytes 524288 | tf_op jit(solution)/shard_map/psum | solution.py:27
  116.3 153.8 %all-gather.2.cloned.1.call-start = ((), (), s32[]{:S(2)}) async-start(), calls=%async_computation.1 | async-start | bytes 2359296 | tf_op jit(solution)/shard_map/all_gather | solution.py:14
  117.0 193.9 %reduce-scatter.2.cloned.1.call-start = ((), (), s32[]{:S(2)}) async-start(), calls=%async_computation.4 | async-start | bytes 1310720 | tf_op jit(solution)/shard_map/reduce_scatter | solution.py:39
  270.1 6.3 %copy-start.1 = (bf16[2048,512]{0,1:T(8,128)(2,1)S(1)}, bf16[2048,512]{0,1:T(8,128)(2,1)}, u32[]{:S(2)}) copy-start(bf16[2048,512]{0,1:T(8,128)(2,1)} %copy.10) | copy-start | bytes 6291460
  270.1 6.3 %copy-start.2 = (bf16[1,2048,512]{1,2,0:T(8,128)(2,1)S(1)}, bf16[1,2048,512]{1,2,0:T(8,128)(2,1)}, u32[]{:S(2)}) copy-start(bf16[1,2048,512]{1,2,0:T(8,128)(2,1)} %copy.11) | copy-start | bytes 6291460
  270.1 6.3 %copy-start.3 = (bf16[1,2048,512]{1,2,0:T(8,128)(2,1)S(1)}, bf16[1,2048,512]{1,2,0:T(8,128)(2,1)}, u32[]{:S(2)}) copy-start(bf16[1,2048,512]{1,2,0:T(8,128)(2,1)} %copy.12) | copy-start | bytes 6291460
  270.1 6.3 %copy-start.4 = (bf16[2048,512]{0,1:T(8,128)(2,1)S(1)}, bf16[2048,512]{0,1:T(8,128)(2,1)}, u32[]{:S(2)}) copy-start(bf16[2048,512]{0,1:T(8,128)(2,1)} %all-gather.2.cloned.1.call-done) | copy-start | bytes 6291460
  279.8 1.3 copy-start.5
Sparse Core Ops, SparseCore 0:
  26.1 58.1 all-reduce.2
  116.4 123.7 all-reduce.4
  241.8 28.1 all-gather.1
  283.6 27.3 reduce-scatter.1
where the time goes:
time: 320 us; the launch traced here: 319 us
  waiting for transfers between devices  230 us (72%)
  matrix products  24.5 us (8%)
  local copies, waits for them, and re-layouts  23.7 us (7%)
  blocking collectives  16 us (5%)
  between operations  13.8 us (4%)
  other arithmetic  11.1 us (3%)
    psum x1, waiting for transfers between devices, on_device(): q_mean = lax.psum(q_raw, ('replica', 'shard')) / replicas  123 us
    psum x1, waiting for transfers between devices, on_device(): p_mean = lax.psum(p_local, 'replica') / replicas  58.3 us
    all_gather x1, waiting for transfers between devices, on_device(): full_momentum = lax.all_gather(momentum, 'replica', axis=1, tiled=True)  29.8 us
    unnamed x20, local copies, waits for them, and re-layouts  22 us
    reduce_scatter x1, waiting for transfers between devices, on_device(): lax.psum_scatter(jnp.dot(own_tokens, new_base, preferred_element_type=jnp...  17.9 us
    psum x1, blocking collectives, on_device(): gram_sum = lax.psum(own_gram, 'shard')  16 us
    dot_general x1, matrix products, on_device(): p_local = jnp.dot(pseudo, q_start, precision=highest)  6.77 us
  transfers between devices with their start and end apart: 4, of which 4 were waited for; matrix products, arithmetic and copies ran while one was open for 3% of the time, Pallas kernels for 0%

commit v1 on v0

--- a/solution.py
+++ b/solution.py
@@ -18,7 +18,7 @@
         + error_feedback[0].astype(jnp.float32)
     )
     p_local = jnp.dot(pseudo, q_start, precision=highest)
-    p_mean = lax.psum(p_local, "replica") / replicas
+    p_mean = jnp.sum(lax.all_gather(p_local, "replica"), axis=0) / replicas
     own_gram = jnp.dot(p_mean.T, p_mean, precision=highest)
     gram_sum = lax.psum(own_gram, "shard")
     factor_low = jnp.linalg.cholesky(gram_sum)

time: 320 us -> 270 us (0.84)
  waiting for transfers between devices: 230 us -> 178 us
    psum x1 -> x0, waiting for transfers between devices: 58.3 us -> none  [on_device(): p_mean = lax.psum(p_local, 'replica') / replicas]
    all_gather x0 -> x1, waiting for transfers between devices: none -> 31.2 us  [on_device(): p_mean = jnp.sum(lax.all_gather(p_local, 'replica'), axis=0) / replicas]
    all_gather x1, waiting for transfers between devices: 29.8 us -> 0.02 us  [on_device(): full_momentum = lax.all_gather(momentum, 'replica', axis=1, tiled=True)]
    psum x1, waiting for transfers between devices: 123 us -> 129 us  [on_device(): q_mean = lax.psum(q_raw, ('replica', 'shard')) / replicas]
    unnamed x20 -> x21, local copies, waits for them, and re-layouts: 22 us -> 24.8 us
  transfers between devices with their start and end apart: 4 -> 4, of which waited for: 4 -> 3; matrix products, arithmetic and copies ran while one was open for 3% -> 10% of each run, Pallas kernels for 0% -> 0%
where the time goes in v1:
time: 270 us; the launch traced here: 269 us
  waiting for transfers between devices  178 us (66%)
  local copies, waits for them, and re-layouts  26.5 us (10%)
  matrix products  22.5 us (8%)
  blocking collectives  16 us (6%)
  between operations  13.8 us (5%)
  other arithmetic  11.7 us (4%)
    psum x1, waiting for transfers between devices, on_device(): q_mean = lax.psum(q_raw, ('replica', 'shard')) / replicas  129 us
    all_gather x1, waiting for transfers between devices, on_device(): p_mean = jnp.sum(lax.all_gather(p_local, 'replica'), axis=0) / replicas  31.2 us
    unnamed x21, local copies, waits for them, and re-layouts  24.8 us
    reduce_scatter x1, waiting for transfers between devices, on_device(): lax.psum_scatter(jnp.dot(own_tokens, new_base, preferred_element_type=jnp...  17.6 us
    psum x1, blocking collectives, on_device(): gram_sum = lax.psum(own_gram, 'shard')  16 us
    dot_general x1, matrix products, on_device(): p_local = jnp.dot(pseudo, q_start, precision=highest)  6.77 us
    dot_general x1, matrix products, on_device(): q_raw = jnp.dot(pseudo.T, basis, precision=highest)  6.42 us
    dot_general x1, matrix products, on_device(): update = jnp.dot(basis, q_mean.T, precision=highest)  6.28 us
  transfers between devices with their start and end apart: 4, of which 3 were waited for; matrix products, arithmetic and copies ran while one was open for 10% of the time, Pallas kernels for 0%

profile of v1, /device:TPU:0, one launch (start us, length us, event | category | flops | bytes accessed | tf_op | source)
XLA Modules:
  0.0 269.1 jit_solution(13298006584807507915)
XLA Ops:
  7.2 0.0 all-gather.6.cloned.1.call-start
  7.2 4.1 %copy.18 = bf16[2048,512]{0,1:T(8,128)(2,1)} copy(bf16[2048,512]{1,0:T(8,128)(2,1)} %param.7) | data formatting | bytes 4194304 | tf_op args[1]
  11.3 4.0 %copy.19 = bf16[1,2048,512]{1,2,0:T(8,128)(2,1)} copy(bf16[1,2048,512]{2,1,0:T(8,128)(2,1)} %param.6) | data formatting | bytes 4194304 | tf_op args[0]
  15.3 3.9 %copy.20 = bf16[1,2048,512]{1,2,0:T(8,128)(2,1)} copy(bf16[1,2048,512]{2,1,0:T(8,128)(2,1)} %param.9) | data formatting | bytes 4194304 | tf_op args[3]
  19.2 6.8 %fusion.10 = f32[2048,32]{0,1:T(8,128)} fusion(f32[512,32]{0,1:T(8,128)S(1)} %copy-done.6, bf16[2048,512]{0,1:T(8,128)(2,1)} %copy.18, bf16[1,2048,512]{1,2,0:T(8,128)(2,1)} %copy.20, bf16[1,2048,512]{1,2,0:T(8,128)(2,1)} %copy.19), kind=kOutput, calls=%fused_computation.12 | convolution fusion | flops 407896064 | bytes 6619136 | tf_op jit(solution)/shard_map/dot_general | solution.py:20
  26.0 0.0 all-gather.4.cloned.1.call-start
  26.1 0.7 all-gather.4.cloned.1.call-update
  26.8 0.0 all-reduce.2.cloned.1.call-start
  26.8 31.2 %all-gather.6.cloned.1.call-done = f32[16384,32]{0,1:T(8,128)} async-done(((f32[2048,32]{0,1:T(8,128)}), f32[16384,32]{0,1:T(8,128)}) %all-gather.6.cloned.1.call-update) | async-done | bytes 2097168 | tf_op jit(solution)/shard_map/all_gather | solution.py:21
  58.0 2.8 %copy.27 = f32[4,8,8,2048]{3,2,1,0:T(8,128)S(1)} copy(f32[4,8,8,2048]{3,1,2,0:T(8,128)} %bitcast.43) | data formatting | bytes 4194304
  60.8 0.5 bitcast_reduce_fusion
  61.4 0.4 fusion.16
  61.7 16.0 %psum.14 = f32[32,32]{0,1:T(8,128)S(1)} all-reduce(f32[32,32]{0,1:T(8,128)S(1)} %fusion.16), channel_id=1, replica_groups=mesh['replica'=8,'shard'=4] {'shard'}, use_global_device_ids=true, to_apply=%region_1.0 | all-reduce | flops 1024 | bytes 8192 | tf_op jit(solution)/shard_map/psum | solution.py:23
  77.7 0.1 copy.22
  77.8 2.9 %cholesky.16 = f32[32,32]{1,0:T(8,128)S(1)} custom-call(f32[32,32]{1,0:T(8,128)S(1)} %fusion.23), custom_call_target="Cholesky" | custom-call | tf_op jit(solution)/shard_map/jit(cholesky)/cholesky | solution.py:24
  80.8 0.6 compare_reduce_fusion
  81.4 0.7 fusion.21
  82.1 2.4 custom-call.7
  84.5 0.4 fusion.14
  84.9 6.4 %fusion.8 = f32[512,32]{1,0:T(8,128)} fusion(f32[32,2048]{1,0:T(8,128)S(1)} %fusion.14, bf16[2048,512]{0,1:T(8,128)(2,1)} %copy.18, bf16[1,2048,512]{1,2,0:T(8,128)(2,1)} %copy.20, bf16[1,2048,512]{1,2,0:T(8,128)(2,1)} %copy.19), kind=kOutput, calls=%fused_computation.11 | convolution fusion | flops 407896064 | bytes 6619136 | tf_op jit(solution)/shard_map/dot_general | solution.py:26
  91.4 0.2 reduce-scatter.2.cloned.1.call-start
  91.6 128.7 %all-reduce.2.cloned.1.call-done = f32[512,32]{1,0:T(8,128)} async-done(((f32[512,32]{1,0:T(8,128)}), f32[512,32]{1,0:T(8,128)}) %all-reduce.2.cloned.1.call-update) | async-done | bytes 65552 | tf_op jit(solution)/shard_map/psum | solution.py:27
  220.3 6.3 %multiply_add_fusion = (bf16[2048,512]{0,1:T(8,128)(2,1)}, f32[2048,512]{0,1:T(8,128)S(1)}) fusion(bf16[2048,512]{0,1:T(8,128)(2,1)} %all-gather.4.cloned.1.call-done, f32[32,2048]{1,0:T(8,128)S(1)} %fusion.14, f32[512,32]{1,0:T(8,128)} %all-reduce.2.cloned.1.call-done), kind=kOutput, calls=%fused_computation.5 | convolution fusion | flops 406863872 | bytes 8716288 | tf_op jit(solution)/shard_map/dot_general | solution.py:28
  226.6 3.5 %fusion.2 = (bf16[1,2048,512]{1,2,0:T(8,128)(2,1)}, bf16[2048,512]{0,1:T(8,128)(2,1)S(1)}) fusion(f32[2048,512]{0,1:T(8,128)S(1)} %get-tuple-element.15, bf16[1,2048,512]{1,2,0:T(8,128)(2,1)S(1)} %copy-done.3, bf16[1,2048,512]{1,2,0:T(8,128)(2,1)S(1)} %copy-done.2, bf16[2048,512]{0,1:T(8,128)(2,1)S(1)} %copy-done.1, bf16[2048,512]{0,1:T(8,128)(2,1)S(1)} %copy-done.4), kind=kLoop, calls=%fused_computation.6 | loop fusion | flops 15728640 | bytes 16777216 | tf_op jit(solution)/shard_map/broadcast_in_dim | solution.py:29
  230.1 1.3 copy-done.5
  231.4 2.3 fusion.5
  233.7 3.9 %copy.23 = bf16[2048,512]{1,0:T(8,128)(2,1)} copy(bf16[2048,512]{0,1:T(8,128)(2,1)} %copy-done.5) | data formatting | bytes 4194304
  237.6 3.9 %copy.24 = bf16[1,2048,512]{2,1,0:T(8,128)(2,1)} copy(bf16[1,2048,512]{1,2,0:T(8,128)(2,1)} %get-tuple-element.12) | data formatting | bytes 4194304
  241.5 1.7 dynamic-slice_convert_fusion
  243.2 17.6 %reduce-scatter.2.cloned.1.call-done = f32[128,512]{0,1:T(8,128)} async-done(((f32[512,512]{0,1:T(8,128)}), f32[128,512]{0,1:T(8,128)}) %reduce-scatter.2.cloned.1.call-update) | async-done | bytes 262160 | tf_op jit(solution)/shard_map/reduce_scatter | solution.py:39
  260.8 1.0 convert_bitcast_fusion
  261.8 0.8 copy.25
  (19 shorter events, 0.1 us)
Async XLA Ops:
  7.2 224.2 %copy-start = (bf16[1,512,2048]{2,1,0:T(8,128)(2,1)S(1)}, bf16[1,512,2048]{2,1,0:T(8,128)(2,1)}, u32[]{:S(2)}) copy-start(bf16[1,512,2048]{2,1,0:T(8,128)(2,1)} %param.11) | copy-start | bytes 6291460
  7.2 50.9 %all-gather.6.cloned.1.call-start = ((), (), s32[]{:S(2)}) async-start(), calls=%async_computation.4 | async-start | bytes 2359296 | tf_op jit(solution)/shard_map/all_gather | solution.py:21
  15.3 3.9 %copy-start.6 = (f32[512,32]{0,1:T(8,128)S(1)}, f32[512,32]{0,1:T(8,128)}, u32[]{:S(2)}) copy-start(f32[512,32]{0,1:T(8,128)} %param.10) | copy-start | bytes 196612
  26.0 65.6 %all-gather.4.cloned.1.call-start = ((), (), s32[]{:S(2)}) async-start(), calls=%async_computation.1 | async-start | bytes 2359296 | tf_op jit(solution)/shard_map/all_gather | solution.py:14
  26.8 193.5 %all-reduce.2.cloned.1.call-start = ((), (), s32[]{:S(2)}) async-start(), calls=%async_computation.2 | async-start | bytes 524288 | tf_op jit(solution)/shard_map/psum | solution.py:27
  91.4 169.4 %reduce-scatter.2.cloned.1.call-start = ((), (), s32[]{:S(2)}) async-start(), calls=%async_computation.3 | async-start | bytes 1310720 | tf_op jit(solution)/shard_map/reduce_scatter | solution.py:39
  220.3 6.3 %copy-start.1 = (bf16[2048,512]{0,1:T(8,128)(2,1)S(1)}, bf16[2048,512]{0,1:T(8,128)(2,1)}, u32[]{:S(2)}) copy-start(bf16[2048,512]{0,1:T(8,128)(2,1)} %copy.18) | copy-start | bytes 6291460
  220.3 6.3 %copy-start.2 = (bf16[1,2048,512]{1,2,0:T(8,128)(2,1)S(1)}, bf16[1,2048,512]{1,2,0:T(8,128)(2,1)}, u32[]{:S(2)}) copy-start(bf16[1,2048,512]{1,2,0:T(8,128)(2,1)} %copy.19) | copy-start | bytes 6291460
  220.3 6.3 %copy-start.3 = (bf16[1,2048,512]{1,2,0:T(8,128)(2,1)S(1)}, bf16[1,2048,512]{1,2,0:T(8,128)(2,1)}, u32[]{:S(2)}) copy-start(bf16[1,2048,512]{1,2,0:T(8,128)(2,1)} %copy.20) | copy-start | bytes 6291460
  220.3 6.3 %copy-start.4 = (bf16[2048,512]{0,1:T(8,128)(2,1)S(1)}, bf16[2048,512]{0,1:T(8,128)(2,1)}, u32[]{:S(2)}) copy-start(bf16[2048,512]{0,1:T(8,128)(2,1)} %all-gather.4.cloned.1.call-done) | copy-start | bytes 6291460
  230.1 1.3 copy-start.5
Sparse Core Ops, SparseCore 0:
  26.1 31.8 all-gather.5
  59.6 28.5 all-gather.3
  94.3 125.9 all-reduce.1
  233.8 26.9 reduce-scatter.1
